TPU v7x, 512 devices: a whole 4x4x16 slice. The times are simulated.
512 devices in a mesh: seq: 32 (over z, core), img: 16 (over y, x).
Axes of the slice: x: 4, y: 4, z: 16, core: 2. Of those that a mesh axis runs over, the one named last changes fastest.
Arguments:
- tokens: bfloat16 [16, 96, 128, 2240], P('img', 'seq'), may hold values from -8 to 8
- norm_gain: bfloat16 [2240], replicated, may hold values from 0.099609375 to 1.8984375
- caption: bfloat16 [16, 2240], P('img'), may hold values from -6 to 6
- null_caption: bfloat16 [2240], replicated, may hold values from -6 to 6
- keep: int32 [16], P('img'), may hold values from 0 to 1, as said below
- bucket_rows: int32 [16], P('img'), may hold values from 25 to 96, as said below
- w_qkv: bfloat16 [2240, 3456], P('img', 'seq'), may hold values from -0.125 to 0.125
Outputs:
- attended: bfloat16 [16, 96, 128, 1152], P('img', 'seq')
Inputs may be any that keep to these rules, and one draw needn't show every extreme that they name: `keep`: 1 keeps the image's caption, 0 drops it; some image keeps and some drops. `bucket_rows`: rows in use are the first ones of an image's grid; some image uses all 96 rows.
All inputs are finite; a program needn't handle non-finite values.
Results may differ from a plain program's by a relative error of at most 0.0017.
Values may be sent and summed in bfloat16 or wider, within the bound.
No kernel may reach another device: no remote copies, remote signals or barrier semaphores. Data moves between devices by JAX's collectives and lax.ppermute only.
A program may use at most 128 MiB of HBM per device.

v0:
```python
import jax
import jax.numpy as jnp
from jax import lax
from jax.sharding import PartitionSpec as P

HDIM = 32
norm_eps = 1e-06
attn_eps = 1e-06


def body(tokens, norm_gain, caption, null_caption, keep, bucket_rows, w_qkv):
    grid_rows = tokens.shape[1]
    grid_cols = tokens.shape[2]
    features_count = tokens.shape[3]
    token_count = grid_rows * grid_cols
    features = tokens.reshape(token_count, features_count).astype(jnp.float32)
    mean_square = jnp.mean(features * features, axis=1, keepdims=True)
    condition = jnp.where(keep[0] > 0, caption[0], null_caption).astype(jnp.float32)
    hidden = (
        features * lax.rsqrt(mean_square + norm_eps) * norm_gain.astype(jnp.float32) + condition
    ).astype(jnp.bfloat16)
    rows_whole = lax.all_gather(w_qkv, "img", axis=0, tiled=True)
    projected = jnp.dot(
        hidden,
        lax.all_gather(rows_whole, "seq", axis=1, tiled=True),
        preferred_element_type=jnp.float32,
    )
    inner_width = projected.shape[1] // 3
    head_count = inner_width // HDIM
    grid_row = (
        lax.axis_index("seq") * grid_rows + jnp.arange(token_count, dtype=jnp.int32) // grid_cols
    )
    live_mask = (grid_row < bucket_rows[0]).astype(jnp.float32)
    queries = jax.nn.relu(projected[:, :inner_width]).reshape(token_count, head_count, HDIM)
    keys_relu = jax.nn.relu(projected[:, inner_width : 2 * inner_width]).reshape(
        token_count, head_count, HDIM
    )
    keys_relu = keys_relu * live_mask[:, None, None]
    values = projected[:, 2 * inner_width :].reshape(token_count, head_count, HDIM)
    state_outer = jnp.einsum("thd,the->hde", keys_relu, values, precision=lax.Precision.HIGHEST)
    key_total = jnp.sum(keys_relu, axis=0)
    state_outer, key_total = lax.psum((state_outer, key_total), "seq")
    numerator = jnp.einsum("thd,hde->the", queries, state_outer, precision=lax.Precision.HIGHEST)
    denominator = jnp.einsum("thd,hd->th", queries, key_total, precision=lax.Precision.HIGHEST)
    result = numerator / (denominator[:, :, None] + attn_eps) * live_mask[:, None, None]
    return result.reshape(1, grid_rows, grid_cols, inner_width).astype(jnp.bfloat16)


def solution(mesh):
    in_specs = (
        P("img", "seq", None, None),
        P(),
        P("img", None),
        P(),
        P("img"),
        P("img"),
        P("img", "seq"),
    )
    out_specs = P("img", "seq", None, None)
    return jax.shard_map(body, mesh=mesh, in_specs=in_specs, out_specs=out_specs, check_vma=False)
```

profile of v0, /device:TPU:2, one launch (start us, length us, event | category | flops | bytes accessed | tf_op | source)
XLA Modules:
  0.0 393.1 jit_solution(5974640022013583326)
XLA Ops:
  6.5 0.0 all-gather.4.cloned.1.call-start
  6.5 27.0 %all-gather = bf16[16,140,108]{2,1,0:T(8,128)(2,1)S(1)} all-gather(bf16[1,140,108]{2,1,0:T(8,128)(2,1)} %bitcast.47), channel_id=1, replica_groups=mesh['seq'=32,'img'=16] {'img'}, dimensions={0}, use_global_device_ids=true | all-gather | bytes 514080 | tf_op jit(solution)/shard_map/all_gather | solution.py:22
  33.6 0.2 reshape.71
  33.8 1.1 copy.18
  34.8 0.0 all-gather.4.cloned.1.call-update
  34.9 0.0 all-reduce.2.cloned.1.call-start
  35.6 2.6 copy.17
  38.8 0.7 convert_element_type.42
  39.5 1.3 reduce.2
  40.9 1.8 multiply_reduce_fusion
  42.7 0.7 select_convert_fusion
  43.4 1.7 fusion.2
  45.1 0.0 copy-start
  45.1 95.0 %all-gather.4.cloned.1.call-done = bf16[32,108,2240]{2,1,0:T(8,128)(2,1)} async-done(((bf16[1,108,2240]{2,1,0:T(8,128)(2,1)}), bf16[32,108,2240]{2,1,0:T(8,128)(2,1)}) %all-gather.4.cloned.1.call-update) | async-done | bytes 15482896 | tf_op jit(solution)/shard_map/all_gather | solution.py:25
  140.1 19.5 %reshape.73 = bf16[3456,2240]{1,0:T(8,128)(2,1)} reshape(bf16[32,108,2240]{2,1,0:T(8,128)(2,1)} %all-gather.4.cloned.1.call-done) | data formatting | bytes 30965760
  159.6 0.0 copy-done
  159.6 10.4 %fusion.17 = f32[384,3456]{1,0:T(8,128)S(1)} fusion(bf16[384,2240]{1,0:T(8,128)(2,1)S(1)} %copy-done, bf16[3456,2240]{1,0:T(8,128)(2,1)} %reshape.73), kind=kOutput, calls=%fused_computation.30 | convolution fusion | flops 5945425920 | bytes 22511616 | tf_op jit(solution)/shard_map/dot_general | solution.py:23
  169.9 2.2 multiply_reduce_fusion.1
  172.1 1.2 copy.19
  173.3 2.2 copy.20
  175.5 3.0 fusion.5
  178.5 0.0 all-reduce.2.cloned.1.call-update
  178.5 2.2 copy.21
  180.7 0.1 reduce_sum.22
  180.8 91.4 %psum.15 = f32[36,32]{1,0:T(8,128)S(1)} all-reduce(f32[36,32]{1,0:T(8,128)S(1)} %reduce_sum.22), channel_id=1, replica_groups=mesh['seq'=32,'img'=16] {'seq'}, use_global_device_ids=true, to_apply=%region_3.4 | all-reduce | flops 1152 | bytes 9216 | tf_op jit(solution)/shard_map/psum | solution.py:42
  272.2 1.1 fusion.9
  273.3 107.9 %all-reduce.2.cloned.1.call-done = f32[36,32,32]{2,1,0:T(8,128)} async-done(((f32[36,32,32]{2,1,0:T(8,128)}), f32[36,32,32]{2,1,0:T(8,128)}) %all-reduce.2.cloned.1.call-update) | async-done | bytes 147472 | tf_op jit(solution)/shard_map/psum | solution.py:42
  381.2 2.8 fusion.4
  384.0 0.3 convert_element_type.47
  384.3 1.9 copy.23
  (3 shorter events, 0.0 us)
Async XLA Ops:
  6.5 133.5 %all-gather.4.cloned.1.call-start = ((), (), s32[]{:S(2)}) async-start(), calls=%async_computation.1 | async-start | bytes 17031168 | tf_op jit(solution)/shard_map/all_gather | solution.py:25
  34.9 346.3 %all-reduce.2.cloned.1.call-start = ((), (), s32[]{:S(2)}) async-start(), calls=%async_computation | async-start | bytes 1179648 | tf_op jit(solution)/shard_map/psum | solution.py:42
  45.1 114.5 %copy-start = (bf16[384,2240]{1,0:T(8,128)(2,1)S(1)}, bf16[384,2240]{1,0:T(8,128)(2,1)}, u32[]{:S(2)}) copy-start(bf16[384,2240]{1,0:T(8,128)(2,1)} %fusion.2) | copy-start | bytes 5160964
Sparse Core Ops, SparseCore 0:
  35.0 105.0 all-gather.3
  178.6 202.5 all-reduce.1
where the time goes:
time: 394 us; the launch traced here: 393 us
  waiting for transfers between devices  203 us (52%)
  blocking collectives  118 us (30%)
  local copies, waits for them, and re-layouts  31.2 us (8%)
  matrix products  17.3 us (4%)
  between operations  14.8 us (4%)
  other arithmetic  8.47 us (2%)
    psum x1, waiting for transfers between devices, body(): state_outer, key_total = lax.psum((state_outer, key_total), 'seq')  108 us
    all_gather x1, waiting for transfers between devices, body(): lax.all_gather(rows_whole, 'seq', axis=1, tiled=True)  95 us
    psum x1, blocking collectives, body(): state_outer, key_total = lax.psum((state_outer, key_total), 'seq')  91.4 us
    all_gather x1, blocking collectives, body(): rows_whole = lax.all_gather(w_qkv, 'img', axis=0, tiled=True)  27 us
    unnamed x5, local copies, waits for them, and re-layouts  20.8 us
    dot_general x1, matrix products, body(): jnp.dot(hidden, lax.all_gather(rows_whole, 'seq', axis=1, tiled=True), pr...  10.4 us
  transfers between devices with their start and end apart: 2, of which 2 were waited for; matrix products, arithmetic and copies ran while one was open for 3% of the time, Pallas kernels for 0%

commit v1 on v0

--- a/solution.py
+++ b/solution.py
@@ -6,6 +6,13 @@
 HDIM = 32
 norm_eps = 1e-06
 attn_eps = 1e-06
+
+
+def _end_pairs_all(inputs):
+    now = jnp.stack([inputs] * lax.axis_size("seq"))
+    g_now = lax.all_to_all(now, axis_name="seq", split_axis=0, concat_axis=0)
+    local_out = jnp.concatenate(g_now, axis=1)
+    return local_out
 
 
 def body(tokens, norm_gain, caption, null_caption, keep, bucket_rows, w_qkv):
@@ -20,11 +27,7 @@
         features * lax.rsqrt(mean_square + norm_eps) * norm_gain.astype(jnp.float32) + condition
     ).astype(jnp.bfloat16)
     rows_whole = lax.all_gather(w_qkv, "img", axis=0, tiled=True)
-    projected = jnp.dot(
-        hidden,
-        lax.all_gather(rows_whole, "seq", axis=1, tiled=True),
-        preferred_element_type=jnp.float32,
-    )
+    projected = jnp.dot(hidden, _end_pairs_all(rows_whole), preferred_element_type=jnp.float32)
     inner_width = projected.shape[1] // 3
     head_count = inner_width // HDIM
     grid_row = (

time: 394 us -> 1020 us (2.59)
  waiting for transfers between devices: 203 us -> 803 us
  starting transfers between devices: 0.04 us -> 12.9 us
  blocking collectives: 118 us -> 129 us
    all_to_all x0 -> x1, waiting for transfers between devices: none -> 700 us  [_end_pairs_all(): g_now = lax.all_to_all(now, axis_name='seq', split_axis=0, concat_axis=0)]
    all_gather x1 -> x0, waiting for transfers between devices: 95 us -> none  [body(): lax.all_gather(rows_whole, 'seq', axis=1, tiled=True)]
    unnamed x5 -> x12, local copies, waits for them, and re-layouts: 20.8 us -> 0.5 us
    reshape x0 -> x1, local copies, waits for them, and re-layouts: none -> 19.6 us  [_end_pairs_all(): local_out = jnp.concatenate(g_now, axis=1)]
    all_to_all x0 -> x1, starting transfers between devices: none -> 12.8 us  [_end_pairs_all(): g_now = lax.all_to_all(now, axis_name='seq', split_axis=0, concat_axis=0)]
    psum x1, blocking collectives: 91.4 us -> 102 us  [body(): state_outer, key_total = lax.psum((state_outer, key_total), 'seq')]
  transfers between devices with their start and end apart: 2 -> 2, of which waited for: 2 -> 2; matrix products, arithmetic and copies ran while one was open for 3% -> 1% of each run, Pallas kernels for 0% -> 0%
where the time goes in v1:
time: 1020 us
  waiting for transfers between devices  803 us (79%)
  blocking collectives  129 us (13%)
  local copies, waits for them, and re-layouts  36.1 us (4%)
  matrix products  17.3 us (2%)
  between operations  14.8 us (1%)
  starting transfers between devices  12.9 us (1%)
    all_to_all x1, waiting for transfers between devices, _end_pairs_all(): g_now = lax.all_to_all(now, axis_name='seq', split_axis=0, concat_axis=0)  700 us
    psum x1, waiting for transfers between devices, body(): state_outer, key_total = lax.psum((state_outer, key_total), 'seq')  103 us
    psum x1, blocking collectives, body(): state_outer, key_total = lax.psum((state_outer, key_total), 'seq')  102 us
    all_gather x1, blocking collectives, body(): rows_whole = lax.all_gather(w_qkv, 'img', axis=0, tiled=True)  27 us
  transfers between devices with their start and end apart: 2, of which 2 were waited for; matrix products, arithmetic and copies ran while one was open for 1% of the time, Pallas kernels for 0%

profile of v1, /device:TPU:2, one launch (start us, length us, event | category | flops | bytes accessed | tf_op | source)
XLA Modules:
  0.0 1016.9 jit_solution(13085250895373773123)
XLA Ops:
  6.5 27.0 %all-gather = bf16[16,140,108]{2,1,0:T(8,128)(2,1)S(1)} all-gather(bf16[1,140,108]{2,1,0:T(8,128)(2,1)} %bitcast.38), channel_id=1, replica_groups=mesh['seq'=32,'img'=16] {'img'}, dimensions={0}, use_global_device_ids=true | all-gather | bytes 514080 | tf_op jit(solution)/shard_map/all_gather | solution.py:29
  33.6 0.2 reshape.90
  33.8 0.3 copy.18
  34.1 5.9 stack.2
  39.9 0.0 copy-start.3
  39.9 0.0 copy-start.2
  39.9 0.0 copy-start
  39.9 12.8 %all-to-all-start = ((bf16[32,2240,108]{1,2,0:T(8,128)(2,1)}), bf16[32,2240,108]{1,2,0:T(8,128)(2,1)}, u32[]{:S(2)}, u32[]{:S(2)}) async-start(bf16[32,2240,108]{1,2,0:T(8,128)(2,1)} %stack.2), calls=%async_computation | async-start | bytes 33030144 | tf_op jit(solution)/shard_map/all_to_all | solution.py:13
  52.8 0.0 copy-start.4
  52.8 0.0 all-reduce.2.cloned.1.call-start
  54.1 0.0 copy-done.3
  54.1 0.0 copy-done.2
  54.2 0.0 copy-done
  54.2 0.3 fusion
  54.6 0.0 copy-done.4
  54.6 1.3 fusion.3
  55.9 2.2 copy.17
  58.2 700.0 %all-to-all-done = bf16[32,2240,108]{1,2,0:T(8,128)(2,1)} async-done(((bf16[32,2240,108]{1,2,0:T(8,128)(2,1)}), bf16[32,2240,108]{1,2,0:T(8,128)(2,1)}, u32[]{:S(2)}, u32[]{:S(2)}) %all-to-all-start) | async-done | bytes 15482912 | tf_op jit(solution)/shard_map/all_to_all | solution.py:13
  758.2 0.0 copy-start.1
  758.2 19.6 %reshape.85 = bf16[2240,3456]{0,1:T(8,128)(2,1)} reshape(bf16[2240,32,108]{0,2,1:T(8,128)(2,1)} %bitcast.3) | data formatting | bytes 30965760 | tf_op jit(solution)/shard_map/reshape | solution.py:14
  777.8 0.0 copy-done.1
  777.8 10.4 %fusion.18 = f32[384,3456]{1,0:T(8,128)S(1)} fusion(bf16[384,2240]{1,0:T(8,128)(2,1)S(1)} %bitcast.36, bf16[2240,3456]{0,1:T(8,128)(2,1)} %reshape.85), kind=kOutput, calls=%fused_computation.31 | convolution fusion | flops 5945425920 | bytes 22511616 | tf_op jit(solution)/shard_map/dot_general | solution.py:30
  788.1 2.2 multiply_reduce_fusion
  790.3 1.2 copy.19
  791.5 2.2 copy.20
  793.7 3.0 fusion.6
  796.7 0.0 all-reduce.2.cloned.1.call-update
  796.7 2.2 copy.21
  798.9 0.1 reduce_sum.22
  799.0 101.6 %psum.15 = f32[36,32]{1,0:T(8,128)S(1)} all-reduce(f32[36,32]{1,0:T(8,128)S(1)} %reduce_sum.22), channel_id=1, replica_groups=mesh['seq'=32,'img'=16] {'seq'}, use_global_device_ids=true, to_apply=%region_3.4 | all-reduce | flops 1152 | bytes 9216 | tf_op jit(solution)/shard_map/psum | solution.py:45
  900.6 1.1 fusion.10
  901.7 103.2 %all-reduce.2.cloned.1.call-done = f32[36,32,32]{2,1,0:T(8,128)} async-done(((f32[36,32,32]{2,1,0:T(8,128)}), f32[36,32,32]{2,1,0:T(8,128)}) %all-reduce.2.cloned.1.call-update) | async-done | bytes 147472 | tf_op jit(solution)/shard_map/psum | solution.py:45
  1005.0 2.8 fusion.5
  1007.8 0.3 convert_element_type.45
  1008.1 1.9 copy.23
  (6 shorter events, 0.1 us)
Async XLA Ops:
  39.9 14.2 %copy-start.3 = (bf16[2240]{0:T(1024)(128)(2,1)S(1)}, bf16[2240]{0:T(1024)(128)(2,1)}, u32[]{:S(2)}) copy-start(bf16[2240]{0:T(1024)(128)(2,1)} %param.8) | copy-start | bytes 13444
  39.9 14.2 %copy-start.2 = (bf16[1,2240]{1,0:T(2,128)(2,1)S(1)}, bf16[1,2240]{1,0:T(2,128)(2,1)}, u32[]{:S(2)}) copy-start(bf16[1,2240]{1,0:T(2,128)(2,1)} %param.9) | copy-start | bytes 13444
  39.9 14.3 %copy-start = (bf16[1,3,128,2240]{2,3,1,0:T(8,128)(2,1)S(1)}, bf16[1,3,128,2240]{2,3,1,0:T(8,128)(2,1)}, u32[]{:S(2)}) copy-start(bf16[1,3,128,2240]{2,3,1,0:T(8,128)(2,1)} %param.7) | copy-start | bytes 5160964
  39.9 718.2 %all-to-all-start = ((bf16[32,2240,108]{1,2,0:T(8,128)(2,1)}), bf16[32,2240,108]{1,2,0:T(8,128)(2,1)}, u32[]{:S(2)}, u32[]{:S(2)}) async-start(bf16[32,2240,108]{1,2,0:T(8,128)(2,1)} %stack.2), calls=%async_computation | async-start | bytes 33030144 | tf_op jit(solution)/shard_map/all_to_all | solution.py:13
  52.8 1.8 copy-start.4
  52.8 952.2 %all-reduce.2.cloned.1.call-start = ((), (), s32[]{:S(2)}) async-start(), calls=%async_computation.1 | async-start | bytes 1179648 | tf_op jit(solution)/shard_map/psum | solution.py:45
  758.2 19.6 %copy-start.1 = (bf16[1,3,128,2240]{3,2,1,0:T(8,128)(2,1)S(1)}, bf16[1,3,128,2240]{3,2,1,0:T(8,128)(2,1)}, u32[]{:S(2)}) copy-start(bf16[1,3,128,2240]{3,2,1,0:T(8,128)(2,1)} %copy.17) | copy-start | bytes 5160964
Sparse Core Ops, SparseCore 0:
  796.9 208.0 all-reduce.1
